TPU v7x, 128 devices: a whole 4x4x4 slice. The times are simulated.
128 devices in a mesh: ctx: 8 (over x, core), head: 16 (over y, z).
Axes of the slice: x: 4, y: 4, z: 4, core: 2. Of those that a mesh axis runs over, the one named last changes fastest.
Arguments:
- queries: bfloat16 [16384, 8192], P(('ctx', 'head')), may hold values from -30 to 30
- keys: bfloat16 [16384, 8192], P(('ctx', 'head')), may hold values from -30 to 30
- values: bfloat16 [16384, 8192], P(('ctx', 'head')), may hold values from -6 to 6
- rates: bfloat16 [16384, 32], P(('ctx', 'head')), may hold values from 0.0009994507 to 0.0099487305
- fast_init: bfloat16 [3, 32, 256, 256], P(None, 'head'), may hold values from -0.375 to 0.375
- gain: float32 [8192], replicated, may hold values from 0.25 to 1.75
Outputs:
- mixed: bfloat16 [16384, 8192], P(('ctx', 'head'))
All inputs are finite; a program needn't handle non-finite values.
Results may differ from a plain program's by a relative error of at most 0.0095.
Values may be sent and summed in bfloat16 or wider, within the bound.
A program may use at most 128 MiB of HBM per device.

v0:
```python
import jax
import jax.numpy as jnp
from jax import lax
from jax.sharding import PartitionSpec as P

WINDOW = 2048


EPSILON = 1e-06


def from_behind(value, axis, steps):
    count = lax.axis_size(axis)
    initial, last = (max(0, -steps), min(count, count - steps))
    return lax.ppermute(value, axis, [(source, source + steps) for source in range(initial, last)])


def carried_in(part, axis, combine, identity):
    place = lax.axis_index(axis)
    gathered = lax.all_gather(part, axis)
    state = jnp.zeros_like(part) + jnp.asarray(identity, part.dtype)

    def one(turn, state):
        return combine(state, lax.dynamic_index_in_dim(gathered, turn, 0, False))

    return lax.fori_loop(0, place, one, state)


def silu_parts(pre):
    sigma = jax.nn.sigmoid(pre)
    return (pre * sigma, sigma)


def add_terms(earlier, later):
    return earlier + later


def on_device(queries, keys, values, rates, fast_init, gain):
    q_rows, k_rows, v_rows, rate_rows = (
        lax.all_to_all(queries, "head", split_axis=1, concat_axis=0, tiled=True),
        lax.all_to_all(keys, "head", split_axis=1, concat_axis=0, tiled=True),
        lax.all_to_all(values, "head", split_axis=1, concat_axis=0, tiled=True),
        lax.all_to_all(rates, "head", split_axis=1, concat_axis=0, tiled=True),
    )
    length = q_rows.shape[0]
    heads_here = fast_init.shape[1]
    head_size = fast_init.shape[3]
    columns = heads_here * head_size
    query_heads = q_rows.reshape(length, heads_here, head_size)
    key_heads = k_rows.reshape(length, heads_here, head_size)
    value_heads = v_rows.reshape(length, heads_here, head_size)
    edge_keys, edge_values = from_behind((k_rows, v_rows), "ctx", 1)
    key_ext = jnp.concatenate([edge_keys, k_rows], 0).reshape(
        WINDOW + length, heads_here, head_size
    )
    value_ext = jnp.concatenate([edge_values, v_rows], 0).reshape(
        WINDOW + length, heads_here, head_size
    )
    anchor = lax.axis_index("ctx") * length
    block = min(512, length)
    scale = head_size ** (-0.5)

    def attend(number):
        start = number * block
        query_block = lax.dynamic_slice_in_dim(query_heads, start, block, 0)
        key_block = lax.dynamic_slice_in_dim(key_ext, start, block + WINDOW, 0)
        value_block = lax.dynamic_slice_in_dim(value_ext, start, block + WINDOW, 0)
        scores = (
            jnp.einsum("qhd,khd->hqk", query_block, key_block, preferred_element_type=jnp.float32)
            * scale
        )
        query_pos = anchor + start + jnp.arange(block, dtype=jnp.int32)[:, None]
        key_pos = anchor + start - WINDOW + jnp.arange(block + WINDOW, dtype=jnp.int32)[None, :]
        valid = ((key_pos <= query_pos) & (key_pos > query_pos - WINDOW) & (key_pos >= 0))[None]
        masked = jnp.where(valid, scores, -jnp.inf)
        top = jnp.max(masked, axis=2, keepdims=True)
        weights = jnp.where(valid, jnp.exp(masked - top), 0.0)
        probs = (weights / jnp.sum(weights, axis=2, keepdims=True)).astype(jnp.bfloat16)
        return jnp.einsum("hqk,khd->qhd", probs, value_block, preferred_element_type=jnp.float32)

    attended = lax.map(attend, jnp.arange(length // block, dtype=jnp.int32)).reshape(
        length, columns
    )
    targets = (rate_rows.astype(jnp.float32)[:, :, None] * value_heads.astype(jnp.float32)).astype(
        jnp.bfloat16
    )
    gate_pre = jnp.einsum(
        "thd,hfd->thf", key_heads, fast_init[0], preferred_element_type=jnp.float32
    )
    up_pre = jnp.einsum("thd,hfd->thf", key_heads, fast_init[1], preferred_element_type=jnp.float32)
    gate_act, sigma = silu_parts(gate_pre)
    hidden = (gate_act * up_pre).astype(jnp.bfloat16)
    back = jnp.einsum("thd,hfd->thf", targets, fast_init[2], preferred_element_type=jnp.float32)
    back_gate = (back * up_pre * sigma * (1.0 + gate_pre * (1.0 - sigma))).astype(jnp.bfloat16)
    back_up = (back * gate_act).astype(jnp.bfloat16)
    totals = jnp.stack(
        [
            jnp.einsum("thf,thd->hfd", back_gate, key_heads, preferred_element_type=jnp.float32),
            jnp.einsum("thf,thd->hfd", back_up, key_heads, preferred_element_type=jnp.float32),
            jnp.einsum("thf,thd->hfd", hidden, targets, preferred_element_type=jnp.float32),
        ]
    )
    zeros = jnp.zeros_like(totals)
    earlier = carried_in(totals, "ctx", add_terms, zeros)
    initial = fast_init.astype(jnp.float32)
    target_ms = jnp.mean(initial * initial, axis=3, keepdims=True)
    renewed = initial + earlier
    current = jnp.mean(renewed * renewed, axis=3, keepdims=True)
    fitted = (renewed * jnp.sqrt(target_ms) * lax.rsqrt(current + EPSILON)).astype(jnp.bfloat16)
    q_gate = jnp.einsum("thd,hfd->thf", query_heads, fitted[0], preferred_element_type=jnp.float32)
    q_up = jnp.einsum("thd,hfd->thf", query_heads, fitted[1], preferred_element_type=jnp.float32)
    q_hidden = (silu_parts(q_gate)[0] * q_up).astype(jnp.bfloat16)
    recalled = jnp.einsum("thf,hfd->thd", q_hidden, fitted[2], preferred_element_type=jnp.float32)
    combined = attended + recalled.reshape(length, columns)
    wide = lax.all_to_all(
        combined.astype(jnp.bfloat16), "head", split_axis=0, concat_axis=1, tiled=True
    ).astype(combined.dtype)
    factor = lax.rsqrt(jnp.mean(wide * wide, axis=1, keepdims=True) + EPSILON)
    result = (wide * factor * gain).astype(jnp.bfloat16)
    return result


def solution(mesh):
    in_specs = (
        P(("ctx", "head"), None),
        P(("ctx", "head"), None),
        P(("ctx", "head"), None),
        P(("ctx", "head"), None),
        P(None, "head", None, None),
        P(),
    )
    out_specs = P(("ctx", "head"), None)
    return jax.shard_map(
        on_device, mesh=mesh, in_specs=in_specs, out_specs=out_specs, check_vma=False
    )
```

profile of v0, /device:TPU:4, one launch (start us, length us, event | category | flops | bytes accessed | tf_op | source)
XLA Modules:
  0.0 409.2 jit_solution(9686523292759929500)
XLA Ops:
  6.5 8.0 %all-to-all-start.3 = ((bf16[128,16,2]{0,2,1:T(2,128)(2,1)}), bf16[128,16,2]{0,2,1:T(2,128)(2,1)S(1)}, u32[]{:S(2)}, u32[]{:S(2)}) async-start(bf16[128,16,2]{0,2,1:T(2,128)(2,1)} %bitcast.170), calls=%async_computation.3 | async-start | bytes 16384 | tf_op jit(solution)/shard_map/all_to_all | solution.py:43
  30.0 25.2 %all-to-all-done.2 = bf16[128,16,512]{0,2,1:T(8,128)(2,1)S(1)} async-done(((bf16[128,16,512]{0,2,1:T(8,128)(2,1)}), bf16[128,16,512]{0,2,1:T(8,128)(2,1)S(1)}, u32[]{:S(2)}, u32[]{:S(2)}) %all-to-all-start.2) | async-done | bytes 2097184 | tf_op jit(solution)/shard_map/all_to_all | solution.py:41
  55.2 4.4 %all-to-all-start = ((bf16[128,16,512]{0,2,1:T(8,128)(2,1)}), bf16[128,16,512]{0,2,1:T(8,128)(2,1)}, u32[]{:S(2)}, u32[]{:S(2)}) async-start(bf16[128,16,512]{0,2,1:T(8,128)(2,1)} %bitcast.161), calls=%async_computation | async-start | bytes 4194304 | tf_op jit(solution)/shard_map/all_to_all | solution.py:42
  71.0 15.7 %all-to-all-done = bf16[128,16,512]{0,2,1:T(8,128)(2,1)} async-done(((bf16[128,16,512]{0,2,1:T(8,128)(2,1)}), bf16[128,16,512]{0,2,1:T(8,128)(2,1)}, u32[]{:S(2)}, u32[]{:S(2)}) %all-to-all-start) | async-done | bytes 2097184 | tf_op jit(solution)/shard_map/all_to_all | solution.py:42
  86.7 4.3 %copy.99 = bf16[16,128,512]{1,0,2:T(8,128)(2,1)} copy(bf16[16,128,512]{1,2,0:T(8,128)(2,1)} %bitcast.8) | data formatting | bytes 4194304 | tf_op jit(solution)/shard_map/all_to_all | solution.py:42
  91.0 4.2 %concatenate.17 = bf16[2048,2,256]{0,2,1:T(8,128)(2,1)} reshape(bf16[16,128,512]{1,0,2:T(8,128)(2,1)} %copy.99) | data formatting | bytes 4194304 | tf_op jit(solution)/shard_map/concatenate | solution.py:56
  98.6 4.2 %fusion.54 = f32[1,2,256,256]{3,2,1,0:T(8,128)S(1)} fusion(bf16[2048,2,256]{0,2,1:T(8,128)(2,1)S(1)} %copy-done.1, f32[2048,2]{0,1:T(2,128)S(1)} %convert_bitcast_fusion.1, f32[2,256,2048]{1,2,0:T(8,128)} %fusion.66, f32[2,256,2048]{1,2,0:T(8,128)S(1)} %copy-done.6), kind=kOutput, calls=%fused_computation.70 | convolution fusion | flops 546308096 | bytes 11026432 | tf_op jit(solution)/shard_map/thf,thd->hfd/dot_general | solution.py:100
  121.4 4.2 %copy.101 = bf16[128,8192]{0,1:T(8,128)(2,1)} copy(bf16[128,8192]{1,0:T(8,128)(2,1)} %param.10) | data formatting | bytes 4194304 | tf_op args[0]
  125.6 4.7 %all-to-all-start.1 = ((bf16[128,16,512]{0,2,1:T(8,128)(2,1)}), bf16[128,16,512]{0,2,1:T(8,128)(2,1)}, u32[]{:S(2)}, u32[]{:S(2)}) async-start(bf16[128,16,512]{0,2,1:T(8,128)(2,1)} %bitcast.162), calls=%async_computation.1 | async-start | bytes 4194304 | tf_op jit(solution)/shard_map/all_to_all | solution.py:40
  130.3 31.3 %all-to-all-done.1 = bf16[128,16,512]{0,2,1:T(8,128)(2,1)} async-done(((bf16[128,16,512]{0,2,1:T(8,128)(2,1)}), bf16[128,16,512]{0,2,1:T(8,128)(2,1)}, u32[]{:S(2)}, u32[]{:S(2)}) %all-to-all-start.1) | async-done | bytes 2097184 | tf_op jit(solution)/shard_map/all_to_all | solution.py:40
  161.6 4.3 %copy.102 = bf16[16,128,512]{1,0,2:T(8,128)(2,1)} copy(bf16[16,128,512]{1,2,0:T(8,128)(2,1)} %bitcast.10) | data formatting | bytes 4194304 | tf_op jit(solution)/shard_map/all_to_all | solution.py:40
  165.8 4.2 %reshape.166 = bf16[2048,2,256]{0,2,1:T(8,128)(2,1)} reshape(bf16[16,128,512]{1,0,2:T(8,128)(2,1)} %copy.102) | data formatting | bytes 4194304 | tf_op jit(solution)/shard_map/reshape | solution.py:49
  170.0 9.1 %collective-permute-done.1 = bf16[2048,512]{1,0:T(8,128)(2,1)} collective-permute-done((bf16[2048,512]{1,0:T(8,128)(2,1)}, bf16[2048,512]{1,0:T(8,128)(2,1)}, u32[]{:S(2)}, u32[]{:S(2)}) %collective-permute-start.1) | collective-permute-done | bytes 2097184 | tf_op jit(solution)/shard_map/ppermute | solution.py:15
  183.1 29.8 %collective-permute-done = bf16[2048,512]{1,0:T(8,128)(2,1)} collective-permute-done((bf16[2048,512]{1,0:T(8,128)(2,1)}, bf16[2048,512]{1,0:T(8,128)(2,1)}, u32[]{:S(2)}, u32[]{:S(2)}) %collective-permute-start) | collective-permute-done | bytes 2097184 | tf_op jit(solution)/shard_map/ppermute | solution.py:15
  216.8 5.5 %pad_maximum_fusion = (bf16[4096,2,256]{0,2,1:T(8,128)(2,1)}, bf16[4096,2,256]{0,2,1:T(8,128)(2,1)}) fusion(bf16[2048,2,256]{0,2,1:T(8,128)(2,1)} %concatenate.17, bf16[2048,2,256]{0,2,1:T(8,128)(2,1)} %bitcast.165, bf16[2048,2,256]{0,2,1:T(8,128)(2,1)S(1)} %concatenate.20, bf16[2048,2,256]{0,2,1:T(8,128)(2,1)} %bitcast.164), kind=kLoop, calls=%fused_computation.30 | loop fusion | flops 16777216 | bytes 16777216 | tf_op jit(solution)/shard_map/concatenate | solution.py:56
  222.3 92.9 %while.23 = (s32[]{:T(128)}, f32[4,512,2,256]{3,2,1,0:T(2,128)}, s32[4]{0:T(128)S(1)}, bf16[4096,2,256]{0,2,1:T(8,128)(2,1)}, s32[]{:T(128)}, /*index=5*/bf16[20...) while((s32[]{:T(128)}, f32[4,512,2,256]{3,2,1,0:T(2,128)}, ...), condition=%wide.region_3.4_spmd, body=%wide.region_0.3_spmd.sunk | while | flops 2707958784 | bytes 35956480 | solution.py:81
  226.5 10.7 %fusion.95 = (f32[2,512]{1,0:T(2,128)S(1)}, f32[2,512,2560]{2,1,0:T(8,128)}) fusion(pred[512,2560]{1,0:T(8,128)(4,1)S(1)} %and_and_fusion.2, bf16[4096,2,256]{0,2,1:T(8,128)(2,1)} %get-tuple-element.308, s32[]{:T(128)S(6)} %select_n.46, bf16[2048,2,256]{0,2,1:T(8,128)(2,1)} %get-tuple-element.307, s32[]{:T(128)S(6)} %select_n.47), kind=kOutput, calls=%fused_computation.93.clone.1 | convolution fusion | flops 1355287040 | bytes 16257032 | tf_op jit(solution)/shard_map/while/body/eval_jaxpr/sub | solution.py:77
  237.2 6.4 %fusion.96 = f32[1,512,2,256]{1,3,2,0:T(8,128)S(1)} fusion(f32[2,512,2560]{2,1,0:T(8,128)} %get-tuple-element.270, f32[2,512]{1,0:T(2,128)S(1)} %get-tuple-element.271, bf16[4096,2,256]{0,2,1:T(8,128)(2,1)} %get-tuple-element.305, s32[]{:T(128)S(6)} %select_n.46), kind=kOutput, calls=%fused_computation.13.clone.1 | convolution fusion | flops 1347420160 | bytes 14159876 | tf_op jit(solution)/shard_map/while/body/eval_jaxpr/hqk,khd->qhd/dot_general | solution.py:79
  249.7 10.7 %fusion.95 = (f32[2,512]{1,0:T(2,128)S(1)}, f32[2,512,2560]{2,1,0:T(8,128)}) fusion(pred[512,2560]{1,0:T(8,128)(4,1)S(1)} %and_and_fusion.2, bf16[4096,2,256]{0,2,1:T(8,128)(2,1)} %get-tuple-element.308, s32[]{:T(128)S(6)} %select_n.46, bf16[2048,2,256]{0,2,1:T(8,128)(2,1)} %get-tuple-element.307, s32[]{:T(128)S(6)} %select_n.47), kind=kOutput, calls=%fused_computation.93.clone.1 | convolution fusion | flops 1355287040 | bytes 16257032 | tf_op jit(solution)/shard_map/while/body/eval_jaxpr/sub | solution.py:77
  260.4 6.4 %fusion.96 = f32[1,512,2,256]{1,3,2,0:T(8,128)S(1)} fusion(f32[2,512,2560]{2,1,0:T(8,128)} %get-tuple-element.270, f32[2,512]{1,0:T(2,128)S(1)} %get-tuple-element.271, bf16[4096,2,256]{0,2,1:T(8,128)(2,1)} %get-tuple-element.305, s32[]{:T(128)S(6)} %select_n.46), kind=kOutput, calls=%fused_computation.13.clone.1 | convolution fusion | flops 1347420160 | bytes 14159876 | tf_op jit(solution)/shard_map/while/body/eval_jaxpr/hqk,khd->qhd/dot_general | solution.py:79
  272.9 10.7 %fusion.95 = (f32[2,512]{1,0:T(2,128)S(1)}, f32[2,512,2560]{2,1,0:T(8,128)}) fusion(pred[512,2560]{1,0:T(8,128)(4,1)S(1)} %and_and_fusion.2, bf16[4096,2,256]{0,2,1:T(8,128)(2,1)} %get-tuple-element.308, s32[]{:T(128)S(6)} %select_n.46, bf16[2048,2,256]{0,2,1:T(8,128)(2,1)} %get-tuple-element.307, s32[]{:T(128)S(6)} %select_n.47), kind=kOutput, calls=%fused_computation.93.clone.1 | convolution fusion | flops 1355287040 | bytes 16257032 | tf_op jit(solution)/shard_map/while/body/eval_jaxpr/sub | solution.py:77
  283.6 6.4 %fusion.96 = f32[1,512,2,256]{1,3,2,0:T(8,128)S(1)} fusion(f32[2,512,2560]{2,1,0:T(8,128)} %get-tuple-element.270, f32[2,512]{1,0:T(2,128)S(1)} %get-tuple-element.271, bf16[4096,2,256]{0,2,1:T(8,128)(2,1)} %get-tuple-element.305, s32[]{:T(128)S(6)} %select_n.46), kind=kOutput, calls=%fused_computation.13.clone.1 | convolution fusion | flops 1347420160 | bytes 14159876 | tf_op jit(solution)/shard_map/while/body/eval_jaxpr/hqk,khd->qhd/dot_general | solution.py:79
  296.1 10.7 %fusion.95 = (f32[2,512]{1,0:T(2,128)S(1)}, f32[2,512,2560]{2,1,0:T(8,128)}) fusion(pred[512,2560]{1,0:T(8,128)(4,1)S(1)} %and_and_fusion.2, bf16[4096,2,256]{0,2,1:T(8,128)(2,1)} %get-tuple-element.308, s32[]{:T(128)S(6)} %select_n.46, bf16[2048,2,256]{0,2,1:T(8,128)(2,1)} %get-tuple-element.307, s32[]{:T(128)S(6)} %select_n.47), kind=kOutput, calls=%fused_computation.93.clone.1 | convolution fusion | flops 1355287040 | bytes 16257032 | tf_op jit(solution)/shard_map/while/body/eval_jaxpr/sub | solution.py:77
  306.8 6.4 %fusion.96 = f32[1,512,2,256]{1,3,2,0:T(8,128)S(1)} fusion(f32[2,512,2560]{2,1,0:T(8,128)} %get-tuple-element.270, f32[2,512]{1,0:T(2,128)S(1)} %get-tuple-element.271, bf16[4096,2,256]{0,2,1:T(8,128)(2,1)} %get-tuple-element.305, s32[]{:T(128)S(6)} %select_n.46), kind=kOutput, calls=%fused_computation.13.clone.1 | convolution fusion | flops 1347420160 | bytes 14159876 | tf_op jit(solution)/shard_map/while/body/eval_jaxpr/hqk,khd->qhd/dot_general | solution.py:79
  315.2 6.4 %reshape.167 = f32[16,128,512]{2,1,0:T(8,128)} reshape(f32[4,512,2,256]{3,2,1,0:T(2,128)} %get-tuple-element.137) | data formatting | bytes 8388608 | tf_op jit(solution)/shard_map/reshape | solution.py:81
  321.8 7.3 %while.24 = (s32[]{:T(128)}, f32[3,2,256,256]{3,2,1,0:T(8,128)S(1)}, s32[]{:T(128)}, f32[8,3,2,256,256]{4,3,2,1,0:T(8,128)}, s32[]{:T(128)}, /*index=5*/s32[]{:T(128)}, s32[]{:T(128)}) while((s32[]{:T(128)}, f32[3,2,256,256]{3,2,1,0:T(8,128)S(1)}, s32[]{:T(128)}, f32[8,3,2,256,256]{4,3,2,1,0:T(8,128)}, s32[]{:T(128)}, /*index=5*/s32[]{:T(128)}, ...), condition=%wide.region_5.6_spmd, body=%wide.region_4.5_spmd.sunk | while | flops 393221 | bytes 4718707 | solution.py:26
  333.6 6.3 %fusion.52 = f32[2,256,2048]{2,1,0:T(8,128)} fusion(f32[2,256,2048]{1,2,0:T(8,128)} %fusion.63, bf16[2048,2,256]{0,2,1:T(8,128)(2,1)S(1)} %copy-done.3, bf16[3,2,256,256]{3,2,1,0:T(8,128)(2,1)S(1)} %multiply_convert_fusion.3), kind=kOutput, calls=%fused_computation.65 | convolution fusion | flops 1080033280 | bytes 11010048 | tf_op jit(solution)/shard_map/thf,hfd->thd/dot_general | solution.py:113
  339.9 5.1 %copy.154 = f32[64,8,16,128]{3,2,1,0:T(8,128)} copy(f32[64,8,16,128]{3,1,2,0:T(8,128)} %bitcast.167) | data formatting | bytes 8388608
  345.0 5.3 %copy.126 = f32[16,128,512]{2,1,0:T(8,128)} copy(f32[16,128,512]{1,0,2:T(8,128)} %bitcast.160) | data formatting | bytes 8388608 | tf_op jit(solution)/shard_map/reshape | solution.py:114
  350.3 4.2 %add_convert_fusion = bf16[16,128,512]{2,1,0:T(8,128)(2,1)S(1)} fusion(f32[16,128,512]{2,1,0:T(8,128)} %reshape.167, f32[16,128,512]{2,1,0:T(8,128)} %copy.126), kind=kLoop, calls=%fused_computation.57 | loop fusion | flops 2097152 | bytes 10485760 | tf_op jit(solution)/shard_map/convert_element_type | solution.py:116
  354.5 33.7 %all_to_all.77 = bf16[16,128,512]{2,1,0:T(8,128)(2,1)S(1)} all-to-all(bf16[16,128,512]{2,1,0:T(8,128)(2,1)S(1)} %add_convert_fusion), channel_id=1, replica_groups=mesh['ctx'=8,'head'=16] {'head'}, dimensions={0} | all-to-all | bytes 4194304 | tf_op jit(solution)/shard_map/all_to_all | solution.py:115
  390.8 5.4 %copy.127 = f32[128,16,512]{0,2,1:T(8,128)} copy(f32[128,16,512]{2,0,1:T(8,128)} %convert_bitcast_fusion) | data formatting | bytes 8388608 | tf_op jit(solution)/shard_map/convert_element_type | solution.py:117
  (84 shorter events, 98.7 us)
Async XLA Ops:
  6.5 15.6 %all-to-all-start.3 = ((bf16[128,16,2]{0,2,1:T(2,128)(2,1)}), bf16[128,16,2]{0,2,1:T(2,128)(2,1)S(1)}, u32[]{:S(2)}, u32[]{:S(2)}) async-start(bf16[128,16,2]{0,2,1:T(2,128)(2,1)} %bitcast.170), calls=%async_computation.3 | async-start | bytes 16384 | tf_op jit(solution)/shard_map/all_to_all | solution.py:43
  22.1 33.1 %all-to-all-start.2 = ((bf16[128,16,512]{0,2,1:T(8,128)(2,1)}), bf16[128,16,512]{0,2,1:T(8,128)(2,1)S(1)}, u32[]{:S(2)}, u32[]{:S(2)}) async-start(bf16[128,16,512]{0,2,1:T(8,128)(2,1)} %bitcast.163), calls=%async_computation.2 | async-start | bytes 4194304 | tf_op jit(solution)/shard_map/all_to_all | solution.py:41
  55.2 4.5 %copy-start = (bf16[128,16,512]{0,2,1:T(8,128)(2,1)}, bf16[128,16,512]{0,2,1:T(8,128)(2,1)S(1)}, u32[]{:S(2)}) copy-start(bf16[128,16,512]{0,2,1:T(8,128)(2,1)S(1)} %all-to-all-done.2) | copy-start | bytes 6291460
  55.2 31.5 %all-to-all-start = ((bf16[128,16,512]{0,2,1:T(8,128)(2,1)}), bf16[128,16,512]{0,2,1:T(8,128)(2,1)}, u32[]{:S(2)}, u32[]{:S(2)}) async-start(bf16[128,16,512]{0,2,1:T(8,128)(2,1)} %bitcast.161), calls=%async_computation | async-start | bytes 4194304 | tf_op jit(solution)/shard_map/all_to_all | solution.py:42
  59.7 262.0 %all-gather.3.cloned.1.call-start = ((), (), s32[]{:S(2)}) async-start(), calls=%async_computation.5 | async-start | bytes 14155776 | tf_op jit(solution)/shard_map/all_gather | solution.py:20
  59.7 5.5 %copy-start.4 = (bf16[3,2,256,256]{3,2,1,0:T(8,128)(2,1)S(1)}, bf16[3,2,256,256]{3,2,1,0:T(8,128)(2,1)}, u32[]{:S(2)}) copy-start(bf16[3,2,256,256]{3,2,1,0:T(8,128)(2,1)} %param.14) | copy-start | bytes 2359300
  95.2 2.7 copy-start.1
  95.2 3.5 copy-start.6
  98.6 4.2 %copy-start.7 = (f32[2,256,2048]{1,2,0:T(8,128)S(1)}, f32[2,256,2048]{1,2,0:T(8,128)}, u32[]{:S(2)}) copy-start(f32[2,256,2048]{1,2,0:T(8,128)} %fusion.66) | copy-start | bytes 12582916
  112.2 66.9 %collective-permute-start.1 = (bf16[2048,512]{1,0:T(8,128)(2,1)}, bf16[2048,512]{1,0:T(8,128)(2,1)}, u32[]{:S(2)}, u32[]{:S(2)}) collective-permute-start(bf16[2048,512]{1,0:T(8,128)(2,1)} %bitcast.168), channel_id=1, source_target_pairs={{0,16},{16,32},{32,48},{48,64},{64,80},{80,96},{96,112},{1,17},{17... | collective-permute-start | bytes 6291464 | tf_op jit(solution)/shard_map/ppermute | solution.py:15
  118.1 94.8 %collective-permute-start = (bf16[2048,512]{1,0:T(8,128)(2,1)}, bf16[2048,512]{1,0:T(8,128)(2,1)}, u32[]{:S(2)}, u32[]{:S(2)}) collective-permute-start(bf16[2048,512]{1,0:T(8,128)(2,1)} %bitcast.169), channel_id=1, source_target_pairs={{0,16},{16,32},{32,48},{48,64},{64,80},{80,96},{96,112},{1,17},{17... | collective-permute-start | bytes 6291464 | tf_op jit(solution)/shard_map/ppermute | solution.py:15
  125.6 36.0 %all-to-all-start.1 = ((bf16[128,16,512]{0,2,1:T(8,128)(2,1)}), bf16[128,16,512]{0,2,1:T(8,128)(2,1)}, u32[]{:S(2)}, u32[]{:S(2)}) async-start(bf16[128,16,512]{0,2,1:T(8,128)(2,1)} %bitcast.162), calls=%async_computation.1 | async-start | bytes 4194304 | tf_op jit(solution)/shard_map/all_to_all | solution.py:40
  321.7 7.4 %copy-start.5 = (bf16[3,2,256,256]{3,2,1,0:T(8,128)(2,1)S(1)}, bf16[3,2,256,256]{3,2,1,0:T(8,128)(2,1)}, u32[]{:S(2)}) copy-start(bf16[3,2,256,256]{3,2,1,0:T(8,128)(2,1)} %param.14) | copy-start | bytes 2359300
  329.1 1.6 copy-start.2
  330.7 2.9 copy-start.3
  390.8 5.9 %copy-start.8 = (f32[8192]{0:T(1024)S(1)}, f32[8192]{0:T(1024)}, u32[]{:S(2)}) copy-start(f32[8192]{0:T(1024)} %param.15) | copy-start | bytes 98308
Sparse Core Ops, SparseCore 0:
  108.4 89.5 all-gather.2
where the time goes:
time: 411 us; the launch traced here: 409 us
  waiting for transfers between devices  115 us (28%)
  matrix products  94.4 us (23%)
  local copies, waits for them, and re-layouts  87.1 us (21%)
  other arithmetic  36.7 us (9%)
  blocking collectives  33.7 us (8%)
  starting transfers between devices  26.2 us (6%)
  between operations  13.6 us (3%)
    sub x4, matrix products, attend(): weights = jnp.where(valid, jnp.exp(masked - top), 0.0)  42.8 us
    ppermute x2, waiting for transfers between devices, from_behind(): lax.ppermute(value, axis, [(source, source + steps) for source in range(i...  38.9 us
    all_to_all x1, blocking collectives, on_device(): lax.all_to_all(combined.astype(jnp.bfloat16), 'head', split_axis=0, conca...  33.7 us
    all_to_all x1, waiting for transfers between devices, on_device(): lax.all_to_all(queries, 'head', split_axis=1, concat_axis=0, tiled=True)  31.3 us
    dot_general x4, matrix products, attend(): jnp.einsum('hqk,khd->qhd', probs, value_block, preferred_element_type=jnp...  25.7 us
    all_to_all x1, waiting for transfers between devices, on_device(): lax.all_to_all(keys, 'head', split_axis=1, concat_axis=0, tiled=True)  25.2 us
    unnamed x22, local copies, waits for them, and re-layouts  18.7 us
    all_to_all x1, waiting for transfers between devices, on_device(): lax.all_to_all(values, 'head', split_axis=1, concat_axis=0, tiled=True)  15.7 us
  transfers between devices with their start and end apart: 7, of which 6 were waited for; matrix products, arithmetic and copies ran while one was open for 37% of the time, Pallas kernels for 0%

commit v1 on v0

v1 whole, which is shorter than its diff:
```python
import functools

import jax
import jax.numpy as jnp
from jax import lax
from jax.experimental import pallas as pl
from jax.experimental.pallas import tpu as pltpu
from jax.sharding import PartitionSpec as P

F32 = jnp.float32
BF16 = jnp.bfloat16
MESH = pl.DeviceIdType.MESH
EPSILON = 1e-06
NT = (((1,), (1,)), ((), ()))
NN = (((1,), (0,)), ((), ()))
TN = (((0,), (0,)), ((), ()))

CTX = 8
PEERS = 16
GROUP = 2048
ROWS = 128
COLS = 512
HD = 256
BLOCK = 256
BLOCKS = GROUP // BLOCK
SLICE = 6 * HD // CTX
SCALE = HD**-0.5 * 1.4426950408889634
LOW = -1e30
SUM_STEP = 1
FIT_STEP = 3

OFFSETS = (
    (0, 1), (1, 0), (0, 3), (3, 0), (1, 1), (3, 3), (1, 3), (3, 1),
    (0, 2), (2, 0), (1, 2), (2, 1), (3, 2), (2, 3), (2, 2),
)


def dot(a, b, dims):
    return lax.dot_general(a, b, dims, preferred_element_type=F32)


def rows_of(index, size, base=0):
    return pl.ds(pl.multiple_of(base + index * size, size), size)


def head_columns(head):
    return slice(head * HD, head * HD + HD)


def attend(block, head, first, q_buf, k_buf, v_buf, s_buf, a_buf):
    cols = head_columns(head)
    here = rows_of(block, BLOCK)
    query = q_buf[here, cols]
    lane = lax.broadcasted_iota(jnp.int32, (BLOCK, HD), 1)
    row = lax.broadcasted_iota(jnp.int32, (BLOCK, HD), 0)
    far = lane > row

    def bias(tile):
        return jnp.where(jnp.logical_and(first, block + tile < BLOCKS), LOW, 0.0).astype(F32)

    def keys(tile):
        return k_buf[rows_of(block + tile, BLOCK), cols]

    def values(tile):
        return v_buf[rows_of(block + tile, BLOCK), cols]

    score = jnp.where(far, dot(query, keys(0), NT) + bias(0), dot(query, keys(BLOCKS), NT))
    s_buf[head, :, 0:HD] = score
    top = jnp.maximum(score[:, :128], score[:, 128:])
    for tile in range(1, BLOCKS):
        score = dot(query, keys(tile), NT)
        s_buf[head, :, tile * HD : tile * HD + HD] = score
        top = jnp.maximum(top, jnp.maximum(score[:, :128], score[:, 128:]) + bias(tile))
    top = jnp.max(top, axis=1, keepdims=True) * SCALE
    prob = jnp.exp2(s_buf[head, :, 0:HD] * SCALE - top)
    total = prob[:, :128] + prob[:, 128:]
    out = dot(jnp.where(far, prob, 0.0).astype(BF16), values(0), NN)
    out = out + dot(jnp.where(far, 0.0, prob).astype(BF16), values(BLOCKS), NN)
    for tile in range(1, BLOCKS):
        prob = jnp.exp2(s_buf[head, :, tile * HD : tile * HD + HD] * SCALE + (bias(tile) * SCALE - top))
        total = total + (prob[:, :128] + prob[:, 128:])
        out = out + dot(prob.astype(BF16), values(tile), NN)
    a_buf[here, cols] = out / jnp.sum(total, axis=1, keepdims=True)


def recall(block, head, q_buf, f_buf, a_buf, o_buf):
    cols = head_columns(head)
    here = rows_of(block, BLOCK)
    query = q_buf[here, cols]
    gate = dot(query, f_buf[head], NT)
    up = dot(query, f_buf[2 + head], NT)
    hidden = (gate * jax.nn.sigmoid(gate) * up).astype(BF16)
    o_buf[here, cols] = (a_buf[here, cols] + dot(hidden, f_buf[4 + head], NN)).astype(BF16)


def update(block, head, k_buf, v_buf, r_buf, w_ref, u_buf):
    cols = head_columns(head)
    here = rows_of(block, BLOCK, GROUP)
    key = k_buf[here, cols]
    value = v_buf[here, cols]
    rate = jnp.concatenate([r_buf[2 * block].T, r_buf[2 * block + 1].T], 0)[:, head : head + 1]
    target = (rate * value.astype(F32)).astype(BF16)
    gate = dot(key, w_ref[0, head], NT)
    up = dot(key, w_ref[1, head], NT)
    back = dot(target, w_ref[2, head], NT)
    sigma = jax.nn.sigmoid(gate)
    act = gate * sigma
    hidden = (act * up).astype(BF16)
    back_gate = (back * up * sigma * (1.0 + gate * (1.0 - sigma))).astype(BF16)
    back_up = (back * act).astype(BF16)
    for part, left, right in ((0, back_gate, key), (1, back_up, key), (2, hidden, target)):
        place = pl.ds((2 * part + head) * HD, HD)
        u_buf[place, :] += dot(left, right, TN)


def fit(part, w_ref, p_buf, f_buf):
    for head in range(2):
        initial = w_ref[part, head].astype(F32)
        renewed = initial + p_buf[pl.ds((2 * part + head) * HD, HD), :].astype(F32)
        wanted = jnp.mean(initial * initial, axis=1, keepdims=True)
        current = jnp.mean(renewed * renewed, axis=1, keepdims=True)
        f_buf[2 * part + head] = (renewed * jnp.sqrt(wanted) * lax.rsqrt(current + EPSILON)).astype(BF16)


def main_kernel(
    q_hbm, k_hbm, v_hbm, r_hbm, w_ref, out_hbm,
    q_buf, k_buf, v_buf, r_buf, s_buf, a_buf, o_buf, u_buf, ub_buf, u_in, p_out, p_buf, f_buf,
    q_in, k_in, v_in, r_in, o_in, q_sent, k_sent, v_sent, r_sent, o_sent,
    fk_in, fv_in, fk_sent, fv_sent, u_got, u_sent, p_got, p_sent,
):
    ctx = lax.axis_index("ctx")
    me = lax.axis_index("head")
    y, z = me // 4, me % 4
    first = ctx == 0
    after = (ctx + 1) % CTX
    peers = [((y + dy) % 4) * 4 + (z + dz) % 4 for dy, dz in OFFSETS]
    lines = [(ctx + step) % CTX for step in range(1, CTX)]

    barrier = pltpu.get_barrier_semaphore()
    for peer in peers:
        pl.semaphore_signal(barrier, inc=1, device_id=(ctx, peer), device_id_type=MESH)
    for line in lines:
        pl.semaphore_signal(barrier, inc=1, device_id=(line, me), device_id_type=MESH)
    pl.semaphore_wait(barrier, len(peers) + len(lines))

    def remote(src, dst, sent, got, where):
        return pltpu.make_async_remote_copy(
            src_ref=src, dst_ref=dst, send_sem=sent, recv_sem=got, device_id=where, device_id_type=MESH
        )

    def columns(ref, peer):
        return ref.at[:, pl.ds(pl.multiple_of(peer * COLS, COLS), COLS)]

    mine = rows_of(me, ROWS)
    mine_late = rows_of(me, ROWS, GROUP)

    def kv_sends(peer):
        return (
            remote(columns(k_hbm, peer), k_buf.at[mine_late], k_sent.at[peer], k_in.at[me], (ctx, peer)),
            remote(columns(v_hbm, peer), v_buf.at[mine_late], v_sent.at[peer], v_in.at[me], (ctx, peer)),
            remote(r_hbm.at[peer], r_buf.at[me], r_sent.at[peer], r_in.at[me], (ctx, peer)),
        )

    def q_send(peer):
        return remote(columns(q_hbm, peer), q_buf.at[mine], q_sent.at[peer], q_in.at[me], (ctx, peer))

    pltpu.make_async_copy(columns(k_hbm, me), k_buf.at[mine_late], k_in.at[me]).start()
    pltpu.make_async_copy(columns(v_hbm, me), v_buf.at[mine_late], v_in.at[me]).start()
    pltpu.make_async_copy(r_hbm.at[me], r_buf.at[me], r_in.at[me]).start()
    for peer in peers:
        for copy in kv_sends(peer):
            copy.start()
    pltpu.make_async_copy(columns(q_hbm, me), q_buf.at[mine], q_in.at[me]).start()
    for peer in peers:
        q_send(peer).start()

    def arrived(ref, sem):
        pltpu.make_async_copy(ref, ref, sem).wait()

    def block_at(step):
        turn = step // 2
        dy = turn + turn // 2 - 2 * (turn // 3)
        return ((y + 4 - dy) % 4) * 2 + (z // 2 + step) % 2

    def forwards(block):
        late, early = rows_of(block, BLOCK, GROUP), rows_of(block, BLOCK)
        return (
            remote(k_buf.at[late], k_buf.at[early], fk_sent.at[block], fk_in.at[block], (after, me)),
            remote(v_buf.at[late], v_buf.at[early], fv_sent.at[block], fv_in.at[block], (after, me)),
        )

    u_buf[...] = jnp.zeros_like(u_buf)

    @pl.loop(0, BLOCKS)
    def _(step):
        block = block_at(step)
        for half in range(2):
            source = 2 * block + half
            here = rows_of(source, ROWS, GROUP)
            arrived(k_buf.at[here], k_in.at[source])
            arrived(v_buf.at[here], v_in.at[source])
            arrived(r_buf.at[source], r_in.at[source])
        for copy in forwards(block):
            copy.start()
        for head in range(2):
            update(block, head, k_buf, v_buf, r_buf, w_ref, u_buf)

    def u_send(line):
        return remote(ub_buf.at[line], u_in.at[ctx], u_sent.at[line], u_got.at[ctx], (line, me))

    def p_send(line):
        return remote(p_out.at[line], p_buf.at[rows_of(ctx, SLICE)], p_sent.at[line], p_got.at[ctx], (line, me))

    for line in range(CTX):
        ub_buf[line] = u_buf[pl.ds(line * SLICE, SLICE), :].astype(BF16)
    for line in lines:
        u_send(line).start()
    u_in[ctx] = ub_buf[ctx]

    @pl.loop(0, BLOCKS)
    def _(block):
        early = rows_of(block, BLOCK)
        arrived(k_buf.at[early], fk_in.at[block])
        arrived(v_buf.at[early], fv_in.at[block])

    def o_send(source):
        here = rows_of(source, ROWS)
        return remote(
            o_buf.at[here], columns(out_hbm, me), o_sent.at[source], o_in.at[me], (ctx, source)
        )

    def o_local():
        return pltpu.make_async_copy(o_buf.at[mine], columns(out_hbm, me), o_in.at[me])

    def finish(block):
        for head in range(2):
            recall(block, head, q_buf, f_buf, a_buf, o_buf)
        for half in range(2):
            source = 2 * block + half

            @pl.when(source == me)
            def _():
                o_local().start()

            @pl.when(source != me)
            def _():
                o_send(source).start()

    @pl.loop(0, BLOCKS)
    def _(step):
        block = block_at(step)
        for half in range(2):
            source = 2 * block + half
            arrived(q_buf.at[rows_of(source, ROWS)], q_in.at[source])
        for head in range(2):
            attend(block, head, first, q_buf, k_buf, v_buf, s_buf, a_buf)

        @pl.when(step == SUM_STEP)
        def _():
            for line in lines:
                arrived(u_in.at[line], u_got.at[line])
            running = jnp.zeros((SLICE, HD), F32)
            for line in range(CTX):
                p_out[line] = running.astype(BF16)
                running = running + u_in[line].astype(F32)
            for line in lines:
                p_send(line).start()
            p_buf[rows_of(ctx, SLICE), :] = p_out[ctx]

        @pl.when(step == FIT_STEP)
        def _():
            for line in lines:
                arrived(p_buf.at[rows_of(line, SLICE)], p_got.at[line])
            for part in range(3):
                fit(part, w_ref, p_buf, f_buf)

            @pl.loop(0, FIT_STEP)
            def _(past):
                finish(block_at(past))

        @pl.when(step >= FIT_STEP)
        def _():
            finish(block)

    for peer in peers:
        for copy in kv_sends(peer):
            copy.wait_send()
        q_send(peer).wait_send()
    for line in lines:
        u_send(line).wait_send()
        p_send(line).wait_send()

    @pl.loop(0, BLOCKS)
    def _(block):
        for copy in forwards(block):
            copy.wait_send()

    for peer in peers:
        o_send(peer).wait_send()
        arrived(columns(out_hbm, peer), o_in.at[peer])
    arrived(columns(out_hbm, me), o_in.at[me])


def norm_kernel(x_ref, gain_ref, out_ref):
    wide = x_ref[...].astype(F32)
    factor = lax.rsqrt(jnp.mean(wide * wide, axis=1, keepdims=True) + EPSILON)
    out_ref[...] = (wide * factor * gain_ref[...]).astype(BF16)


def on_device(queries, keys, values, rates, fast_init, gain):
    rate_rows = jnp.pad(rates.astype(F32).T.reshape(PEERS, 2, ROWS), ((0, 0), (0, 6), (0, 0)))
    anywhere = pl.BlockSpec(memory_space=pl.ANY)
    near = pl.BlockSpec(memory_space=pltpu.VMEM)
    dma = pltpu.SemaphoreType.DMA
    wide = pl.pallas_call(
        main_kernel,
        out_shape=jax.ShapeDtypeStruct((ROWS, PEERS * COLS), BF16),
        in_specs=[anywhere, anywhere, anywhere, anywhere, near],
        out_specs=anywhere,
        scratch_shapes=[
            pltpu.VMEM((GROUP, COLS), BF16),
            pltpu.VMEM((2 * GROUP, COLS), BF16),
            pltpu.VMEM((2 * GROUP, COLS), BF16),
            pltpu.VMEM((PEERS, 8, ROWS), F32),
            pltpu.VMEM((2, BLOCK, GROUP), F32),
            pltpu.VMEM((GROUP, COLS), F32),
            pltpu.VMEM((GROUP, COLS), BF16),
            pltpu.VMEM((6 * HD, HD), F32),
            pltpu.VMEM((CTX, SLICE, HD), BF16),
            pltpu.VMEM((CTX, SLICE, HD), BF16),
            pltpu.VMEM((CTX, SLICE, HD), BF16),
            pltpu.VMEM((6 * HD, HD), BF16),
            pltpu.VMEM((6, HD, HD), BF16),
        ]
        + [dma((PEERS,))] * 10
        + [dma((BLOCKS,))] * 4
        + [dma((CTX,))] * 4,
        compiler_params=pltpu.CompilerParams(
            collective_id=0, has_side_effects=True, vmem_limit_bytes=48 * 2**20
        ),
        name="layer",
    )(queries, keys, values, rate_rows, fast_init)
    tile = 32
    return pl.pallas_call(
        norm_kernel,
        grid=(ROWS // tile,),
        out_shape=jax.ShapeDtypeStruct((ROWS, PEERS * COLS), BF16),
        in_specs=[
            pl.BlockSpec((tile, PEERS * COLS), lambda i: (i, 0)),
            pl.BlockSpec((1, PEERS * COLS), lambda i: (0, 0)),
        ],
        out_specs=pl.BlockSpec((tile, PEERS * COLS), lambda i: (i, 0)),
        name="norm",
    )(wide, gain.reshape(1, -1))


def solution(mesh):
    rows = P(("ctx", "head"), None)
    return jax.shard_map(
        on_device,
        mesh=mesh,
        in_specs=(rows, rows, rows, rows, P(None, "head", None, None), P()),
        out_specs=rows,
        check_vma=False,
    )
```

time: 411 us -> 157 us (0.38)
  the two profiles are of different devices: /device:TPU:4 before, /device:TPU:105 now
where the time goes in v1:
time: 157 us
  Pallas kernels  152 us (97%)
  local copies, waits for them, and re-layouts  4.05 us (3%)
    pallas_call x1, Pallas kernels, on_device(): pl.pallas_call(main_kernel, out_shape=jax.ShapeDtypeStruct((ROWS, PEERS *...  148 us
    pallas_call x1, Pallas kernels, on_device(): pl.pallas_call(norm_kernel, grid=(ROWS // tile,), out_shape=jax.ShapeDtyp...  4.36 us
    unnamed x6, local copies, waits for them, and re-layouts  4.05 us

profile of v1, /device:TPU:105, one launch (start us, length us, event | category | flops | bytes accessed | tf_op | source)
XLA Modules:
  0.0 157.2 jit_solution(1972728451327119689)
XLA Ops:
  0.0 0.7 pad_convert_fusion.r_hbm
  0.7 0.0 copy-start.1
  0.7 1.6 %copy-done.1 = bf16[128,8192]{1,0:T(8,128)(2,1)S(1)} copy-done((bf16[128,8192]{1,0:T(8,128)(2,1)S(1)}, bf16[128,8192]{1,0:T(8,128)(2,1)}, u32[]{:S(2)}) %copy-start.1) | copy-done | bytes 2097176
  2.3 0.0 copy-start.2
  2.3 1.1 copy-done.2
  3.4 148.0 %layer.1.x_ref = bf16[128,8192]{1,0:T(8,128)(2,1)S(1)} custom-call(bf16[128,8192]{1,0:T(8,128)(2,1)S(1)} %copy-done.1, bf16[128,8192]{1,0:T(8,128)(2,1)} %k_hbm.1, bf16[128,8192]{1,0:T(8,128)(2,1)} %v_hbm.1, f32[16,8,128]{2,1,0:T(8,128)S(1)} %pad_convert_fusion.r_hbm, bf16[3,2,256,256]{3,2,1,0:T(8,128)(2,1)S(1)} %copy-done.2), custom_call_target="tpu_custom_call" | custom-call | tf_op jit(solution)/shard_map/layer/pallas_call | solution.py:315
  151.5 0.0 copy-start
  151.5 1.3 copy-done
  152.8 4.4 %norm.1 = bf16[128,8192]{1,0:T(8,128)(2,1)} custom-call(bf16[128,8192]{1,0:T(8,128)(2,1)} %copy-done, f32[1,8192]{1,0:T(1,128)} %bitcast.4), custom_call_target="tpu_custom_call" | custom-call | tf_op jit(solution)/shard_map/norm/pallas_call | solution.py:344
Async XLA Ops:
  0.7 1.6 %copy-start.1 = (bf16[128,8192]{1,0:T(8,128)(2,1)S(1)}, bf16[128,8192]{1,0:T(8,128)(2,1)}, u32[]{:S(2)}) copy-start(bf16[128,8192]{1,0:T(8,128)(2,1)} %q_hbm.1) | copy-start | bytes 6291460
  2.3 1.1 copy-start.2
  151.5 1.3 copy-start

commit v2 on v1

--- a/solution.py
+++ b/solution.py
@@ -29,10 +29,13 @@
 SUM_STEP = 1
 FIT_STEP = 3
 
+TURNS = (1, 3, 2)
+
 OFFSETS = (
     (0, 1), (1, 0), (0, 3), (3, 0), (1, 1), (3, 3), (1, 3), (3, 1),
     (0, 2), (2, 0), (1, 2), (2, 1), (3, 2), (2, 3), (2, 2),
 )
+SLOTS = ((1, 1), (3, 1), (1, 3), (3, 3), (1, 2), (3, 2), (2, 1), (2, 3), (2, 2))
 
 
 def dot(a, b, dims):
@@ -124,9 +127,9 @@
 
 def main_kernel(
     q_hbm, k_hbm, v_hbm, r_hbm, w_ref, out_hbm,
-    q_buf, k_buf, v_buf, r_buf, s_buf, a_buf, o_buf, u_buf, ub_buf, u_in, p_out, p_buf, f_buf,
+    q_buf, k_buf, v_buf, t_buf, r_buf, s_buf, a_buf, o_buf, u_buf, ub_buf, u_in, p_out, p_buf, f_buf,
     q_in, k_in, v_in, r_in, o_in, q_sent, k_sent, v_sent, r_sent, o_sent,
-    fk_in, fv_in, fk_sent, fv_sent, u_got, u_sent, p_got, p_sent,
+    fk_in, fv_in, fk_sent, fv_sent, t_in, tk_sent, tv_sent, ak_sent, av_sent, u_got, u_sent, p_got, p_sent,
 ):
     ctx = lax.axis_index("ctx")
     me = lax.axis_index("head")
@@ -154,11 +157,33 @@
     mine = rows_of(me, ROWS)
     mine_late = rows_of(me, ROWS, GROUP)
 
+    def device_at(dy, dz):
+        return ((y + dy + 4) % 4) * 4 + (z + dz + 4) % 4
+
     def kv_sends(peer):
         return (
             remote(columns(k_hbm, peer), k_buf.at[mine_late], k_sent.at[peer], k_in.at[me], (ctx, peer)),
             remote(columns(v_hbm, peer), v_buf.at[mine_late], v_sent.at[peer], v_in.at[me], (ctx, peer)),
-            remote(r_hbm.at[peer], r_buf.at[me], r_sent.at[peer], r_in.at[me], (ctx, peer)),
+        )
+
+    def r_send(peer):
+        return remote(r_hbm.at[peer], r_buf.at[me], r_sent.at[peer], r_in.at[me], (ctx, peer))
+
+    def slot_sends(slot):
+        dz, dy = SLOTS[slot]
+        peer, way = device_at(dy, dz), device_at(0, dz)
+        return (
+            remote(columns(k_hbm, peer), t_buf.at[slot, 0], tk_sent.at[slot], t_in.at[slot], (ctx, way)),
+            remote(columns(v_hbm, peer), t_buf.at[slot, 1], tv_sent.at[slot], t_in.at[slot], (ctx, way)),
+        )
+
+    def relays(slot):
+        dz, dy = SLOTS[slot]
+        source, peer = device_at(0, -dz), device_at(dy, 0)
+        there = rows_of(source, ROWS, GROUP)
+        return (
+            remote(t_buf.at[slot, 0], k_buf.at[there], ak_sent.at[slot], k_in.at[source], (ctx, peer)),
+            remote(t_buf.at[slot, 1], v_buf.at[there], av_sent.at[slot], v_in.at[source], (ctx, peer)),
         )
 
     def q_send(peer):
@@ -168,42 +193,108 @@
     pltpu.make_async_copy(columns(v_hbm, me), v_buf.at[mine_late], v_in.at[me]).start()
     pltpu.make_async_copy(r_hbm.at[me], r_buf.at[me], r_in.at[me]).start()
     for peer in peers:
+        r_send(peer).start()
+    straight = [device_at(dy, 0) for dy in TURNS] + [device_at(0, dz) for dz in TURNS]
+    for peer in straight[:3]:
         for copy in kv_sends(peer):
             copy.start()
+    for slot in range(6):
+        for copy in slot_sends(slot):
+            copy.start()
+    for peer in straight[3:5]:
+        for copy in kv_sends(peer):
+            copy.start()
+    for slot in range(6, len(SLOTS)):
+        for copy in slot_sends(slot):
+            copy.start()
+    for copy in kv_sends(straight[5]):
+        copy.start()
+
+    def arrived(ref, sem):
+        pltpu.make_async_copy(ref, ref, sem).wait()
+
+    def turn_at(step):
+        late = (step + 6) // 8
+        far = step // 6
+        spot = step % 2
+        dy = late * ((1 + 2 * spot) * (1 - far) + 2 * far)
+        other = (1 - late + far) * spot + (step // 4) * (1 - far)
+        return dy, other
+
+    def block_at(step):
+        dy, other = turn_at(step)
+        return ((y + 4 - dy) % 4) * 2 + (z // 2 + other) % 2
+
+    q_peers = []
+    for step in range(BLOCKS - 1):
+        dy, other = turn_at(step)
+        pair = ((y + dy) % 4) * 4 + 2 * ((z // 2 + other) % 2)
+        q_peers += [pair, pair + 1]
+    q_peers.append(y * 4 + z + 1 - 2 * (z % 2))
+
+    def forwards(source):
+        late, early = rows_of(source, ROWS, GROUP), rows_of(source, ROWS)
+        return (
+            remote(k_buf.at[late], k_buf.at[early], fk_sent.at[source], fk_in.at[source], (after, me)),
+            remote(v_buf.at[late], v_buf.at[early], fv_sent.at[source], fv_in.at[source], (after, me)),
+        )
+
+    def forward(dy, dz):
+        source = device_at(-dy, dz)
+        late = rows_of(source, ROWS, GROUP)
+        arrived(k_buf.at[late], k_in.at[source])
+        arrived(v_buf.at[late], v_in.at[source])
+        arrived(r_buf.at[source], r_in.at[source])
+        for copy in forwards(source):
+            copy.start()
+
+    def relay(slot):
+        arrived(t_buf.at[slot], t_in.at[slot])
+        for copy in relays(slot):
+            copy.start()
+
+    def updates(dy, other):
+        block = ((y + 4 - dy) % 4) * 2 + (z // 2 + other) % 2
+        for head in range(2):
+            update(block, head, k_buf, v_buf, r_buf, w_ref, u_buf)
+
+    forward(0, 0)
+    u_buf[...] = jnp.zeros_like(u_buf)
+    relay(0)
+    relay(1)
+    forward(1, 0)
+    forward(3, 0)
+    relay(2)
+    relay(3)
+    forward(2, 0)
+    relay(4)
+    relay(5)
+    forward(1, -1)
+    forward(3, -1)
+    forward(0, -1)
+    forward(0, 1)
+    updates(0, 0)
+    forward(1, 1)
+    forward(3, 1)
+    updates(1, 0)
+    relay(6)
+    updates(3, 0)
+    relay(7)
+    forward(2, -1)
+    relay(8)
     pltpu.make_async_copy(columns(q_hbm, me), q_buf.at[mine], q_in.at[me]).start()
     for peer in peers:
         q_send(peer).start()
-
-    def arrived(ref, sem):
-        pltpu.make_async_copy(ref, ref, sem).wait()
-
-    def block_at(step):
-        turn = step // 2
-        dy = turn + turn // 2 - 2 * (turn // 3)
-        return ((y + 4 - dy) % 4) * 2 + (z // 2 + step) % 2
-
-    def forwards(block):
-        late, early = rows_of(block, BLOCK, GROUP), rows_of(block, BLOCK)
-        return (
-            remote(k_buf.at[late], k_buf.at[early], fk_sent.at[block], fk_in.at[block], (after, me)),
-            remote(v_buf.at[late], v_buf.at[early], fv_sent.at[block], fv_in.at[block], (after, me)),
-        )
-
-    u_buf[...] = jnp.zeros_like(u_buf)
-
-    @pl.loop(0, BLOCKS)
-    def _(step):
-        block = block_at(step)
-        for half in range(2):
-            source = 2 * block + half
-            here = rows_of(source, ROWS, GROUP)
-            arrived(k_buf.at[here], k_in.at[source])
-            arrived(v_buf.at[here], v_in.at[source])
-            arrived(r_buf.at[source], r_in.at[source])
-        for copy in forwards(block):
-            copy.start()
-        for head in range(2):
-            update(block, head, k_buf, v_buf, r_buf, w_ref, u_buf)
+    forward(2, 1)
+    updates(2, 0)
+    forward(1, 2)
+    updates(1, 1)
+    forward(3, 2)
+    updates(3, 1)
+    forward(2, 2)
+    updates(2, 1)
+    forward(0, 2)
+    updates(0, 1)
 
     def u_send(line):
         return remote(ub_buf.at[line], u_in.at[ctx], u_sent.at[line], u_got.at[ctx], (line, me))
@@ -217,11 +308,11 @@
         u_send(line).start()
     u_in[ctx] = ub_buf[ctx]
 
-    @pl.loop(0, BLOCKS)
-    def _(block):
-        early = rows_of(block, BLOCK)
-        arrived(k_buf.at[early], fk_in.at[block])
-        arrived(v_buf.at[early], fv_in.at[block])
+    @pl.loop(0, PEERS)
+    def _(source):
+        early = rows_of(source, ROWS)
+        arrived(k_buf.at[early], fk_in.at[source])
+        arrived(v_buf.at[early], fv_in.at[source])
 
     def o_send(source):
         here = rows_of(source, ROWS)
@@ -282,17 +373,22 @@
         def _():
             finish(block)
 
-    for peer in peers:
+    for peer in straight:
         for copy in kv_sends(peer):
             copy.wait_send()
+    for slot in range(len(SLOTS)):
+        for copy in slot_sends(slot) + relays(slot):
+            copy.wait_send()
+    for peer in peers:
+        r_send(peer).wait_send()
         q_send(peer).wait_send()
     for line in lines:
         u_send(line).wait_send()
         p_send(line).wait_send()
 
-    @pl.loop(0, BLOCKS)
-    def _(block):
-        for copy in forwards(block):
+    @pl.loop(0, PEERS)
+    def _(source):
+        for copy in forwards(source):
             copy.wait_send()
 
     for peer in peers:
@@ -321,6 +417,7 @@
             pltpu.VMEM((GROUP, COLS), BF16),
             pltpu.VMEM((2 * GROUP, COLS), BF16),
             pltpu.VMEM((2 * GROUP, COLS), BF16),
+            pltpu.VMEM((len(SLOTS), 2, ROWS, COLS), BF16),
             pltpu.VMEM((PEERS, 8, ROWS), F32),
             pltpu.VMEM((2, BLOCK, GROUP), F32),
             pltpu.VMEM((GROUP, COLS), F32),
@@ -333,10 +430,11 @@
             pltpu.VMEM((6, HD, HD), BF16),
         ]
         + [dma((PEERS,))] * 10
-        + [dma((BLOCKS,))] * 4
+        + [dma((PEERS,))] * 4
+        + [dma((len(SLOTS),))] * 5
         + [dma((CTX,))] * 4,
         compiler_params=pltpu.CompilerParams(
-            collective_id=0, has_side_effects=True, vmem_limit_bytes=48 * 2**20
+            collective_id=0, has_side_effects=True, vmem_limit_bytes=60 * 2**20
         ),
         name="layer",
     )(queries, keys, values, rate_rows, fast_init)

time: 157 us -> 131 us (0.83)
  the two profiles are of different devices: /device:TPU:105 before, /device:TPU:4 now
where the time goes in v2:
time: 131 us; the launch traced here: 129 us
  Pallas kernels  128 us (98%)
  other arithmetic  1.33 us (1%)
    pallas_call x1, Pallas kernels, on_device(): pl.pallas_call(main_kernel, out_shape=jax.ShapeDtypeStruct((ROWS, PEERS *...  124 us
    pallas_call x1, Pallas kernels, on_device(): pl.pallas_call(norm_kernel, grid=(ROWS // tile,), out_shape=jax.ShapeDtyp...  4.37 us

profile of v2, /device:TPU:4, one launch (start us, length us, event | category | flops | bytes accessed | tf_op | source)
XLA Modules:
  0.0 129.4 jit_solution(11026458075273754042)
XLA Ops:
  0.0 1.3 %pad_convert_fusion.r_hbm = f32[16,8,128]{2,1,0:T(8,128)} fusion(bf16[16,2,128]{2,1,0:T(2,128)(2,1)} %bitcast.5), kind=kLoop, calls=%fused_computation | loop fusion | flops 16384 | bytes 73728 | tf_op jit(solution)/shard_map/jit(_pad)/pad | solution.py:407
  1.3 123.7 %layer.1.x_ref = bf16[128,8192]{1,0:T(8,128)(2,1)} custom-call(bf16[128,8192]{1,0:T(8,128)(2,1)} %q_hbm.1, bf16[128,8192]{1,0:T(8,128)(2,1)} %k_hbm.1, bf16[128,8192]{1,0:T(8,128)(2,1)} %v_hbm.1, f32[16,8,128]{2,1,0:T(8,128)} %pad_convert_fusion.r_hbm, bf16[3,2,256,256]{3,2,1,0:T(8,128)(2,1)} %w_ref.1), custom_call_target="tpu_custom_call" | custom-call | tf_op jit(solution)/shard_map/layer/pallas_call | solution.py:411
  125.1 4.4 %norm.1 = bf16[128,8192]{1,0:T(8,128)(2,1)} custom-call(bf16[128,8192]{1,0:T(8,128)(2,1)} %layer.1.x_ref, f32[1,8192]{1,0:T(1,128)} %bitcast.4), custom_call_target="tpu_custom_call" | custom-call | tf_op jit(solution)/shard_map/norm/pallas_call | solution.py:442

commit v3 on v2

--- a/solution.py
+++ b/solution.py
@@ -35,6 +35,7 @@
     (0, 1), (1, 0), (0, 3), (3, 0), (1, 1), (3, 3), (1, 3), (3, 1),
     (0, 2), (2, 0), (1, 2), (2, 1), (3, 2), (2, 3), (2, 2),
 )
+FAR = ((1, 1), (3, 3), (1, 3), (3, 1), (0, 2), (1, 2), (3, 2), (2, 0), (2, 1), (2, 3), (2, 2))
 SLOTS = ((1, 1), (3, 1), (1, 3), (3, 3), (1, 2), (3, 2), (2, 1), (2, 3), (2, 2))
 
 
@@ -127,9 +128,9 @@
 
 def main_kernel(
     q_hbm, k_hbm, v_hbm, r_hbm, w_ref, out_hbm,
-    q_buf, k_buf, v_buf, t_buf, r_buf, s_buf, a_buf, o_buf, u_buf, ub_buf, u_in, p_out, p_buf, f_buf,
-    q_in, k_in, v_in, r_in, o_in, q_sent, k_sent, v_sent, r_sent, o_sent,
-    fk_in, fv_in, fk_sent, fv_sent, t_in, tk_sent, tv_sent, ak_sent, av_sent, u_got, u_sent, p_got, p_sent,
+    q_buf, k_buf, v_buf, t_buf, rt_buf, r_buf, s_buf, a_buf, o_buf, o_in_slot, u_buf, ub_buf, u_in, p_out, p_buf, f_buf,
+    q_in, k_in, v_in, o_in, q_sent, k_sent, v_sent, o_sent, rt_in, rt_sent, r_in, r_sent,
+    fk_in, fv_in, fk_sent, fv_sent, t_in, tv_in, tk_sent, tv_sent, ak_sent, av_sent, ot_in, ot_sent, oa_sent, u_got, u_sent, p_got, p_sent,
 ):
     ctx = lax.axis_index("ctx")
     me = lax.axis_index("head")
@@ -166,15 +167,20 @@
             remote(columns(v_hbm, peer), v_buf.at[mine_late], v_sent.at[peer], v_in.at[me], (ctx, peer)),
         )
 
-    def r_send(peer):
-        return remote(r_hbm.at[peer], r_buf.at[me], r_sent.at[peer], r_in.at[me], (ctx, peer))
+    def r_aside(dz):
+        way = (z + dz) % 4
+        return remote(r_hbm.at[:, way], rt_buf.at[z], rt_sent.at[dz], rt_in.at[z], (ctx, y * 4 + way))
+
+    def r_relay(dy):
+        way = (y + dy) % 4
+        return remote(rt_buf.at[:, way], r_buf.at[rows_of(y, 4)], r_sent.at[dy], r_in.at[y], (ctx, way * 4 + z))
 
     def slot_sends(slot):
         dz, dy = SLOTS[slot]
         peer, way = device_at(dy, dz), device_at(0, dz)
         return (
             remote(columns(k_hbm, peer), t_buf.at[slot, 0], tk_sent.at[slot], t_in.at[slot], (ctx, way)),
-            remote(columns(v_hbm, peer), t_buf.at[slot, 1], tv_sent.at[slot], t_in.at[slot], (ctx, way)),
+            remote(columns(v_hbm, peer), t_buf.at[slot, 1], tv_sent.at[slot], tv_in.at[slot], (ctx, way)),
         )
 
     def relays(slot):
@@ -191,9 +197,9 @@
 
     pltpu.make_async_copy(columns(k_hbm, me), k_buf.at[mine_late], k_in.at[me]).start()
     pltpu.make_async_copy(columns(v_hbm, me), v_buf.at[mine_late], v_in.at[me]).start()
-    pltpu.make_async_copy(r_hbm.at[me], r_buf.at[me], r_in.at[me]).start()
-    for peer in peers:
-        r_send(peer).start()
+    pltpu.make_async_copy(r_hbm.at[:, z], rt_buf.at[z], rt_in.at[z]).start()
+    for dz in TURNS:
+        r_aside(dz).start()
     straight = [device_at(dy, 0) for dy in TURNS] + [device_at(0, dz) for dz in TURNS]
     for peer in straight[:3]:
         for copy in kv_sends(peer):
@@ -204,33 +210,23 @@
     for peer in straight[3:5]:
         for copy in kv_sends(peer):
             copy.start()
-    for slot in range(6, len(SLOTS)):
-        for copy in slot_sends(slot):
-            copy.start()
-    for copy in kv_sends(straight[5]):
-        copy.start()
 
     def arrived(ref, sem):
         pltpu.make_async_copy(ref, ref, sem).wait()
 
     def turn_at(step):
-        late = (step + 6) // 8
-        far = step // 6
-        spot = step % 2
-        dy = late * ((1 + 2 * spot) * (1 - far) + 2 * far)
-        other = (1 - late + far) * spot + (step // 4) * (1 - far)
-        return dy, other
+        last = step // 6
+        far = step // 4 - last
+        near = 1 - far - last
+        dy = near * (1 + 2 * (step % 2)) + 2 * far
+        return dy, near * (step // 2) + far * (step % 2) + last * (1 - step % 2)
 
     def block_at(step):
         dy, other = turn_at(step)
         return ((y + 4 - dy) % 4) * 2 + (z // 2 + other) % 2
 
-    q_peers = []
-    for step in range(BLOCKS - 1):
-        dy, other = turn_at(step)
-        pair = ((y + dy) % 4) * 4 + 2 * ((z // 2 + other) % 2)
-        q_peers += [pair, pair + 1]
-    q_peers.append(y * 4 + z + 1 - 2 * (z % 2))
+    near_peers = [device_at(*turn) for turn in ((1, 0), (3, 0), (0, 1), (0, 3))]
+    far_peers = [device_at(*turn) for turn in FAR]
 
     def forwards(source):
         late, early = rows_of(source, ROWS, GROUP), rows_of(source, ROWS)
@@ -244,14 +240,18 @@
         late = rows_of(source, ROWS, GROUP)
         arrived(k_buf.at[late], k_in.at[source])
         arrived(v_buf.at[late], v_in.at[source])
-        arrived(r_buf.at[source], r_in.at[source])
         for copy in forwards(source):
             copy.start()
 
-    def relay(slot):
-        arrived(t_buf.at[slot], t_in.at[slot])
-        for copy in relays(slot):
-            copy.start()
+    def relay(slot, *more):
+        for part, sem in ((0, t_in), (1, tv_in)):
+            for each in (slot,) + more:
+                arrived(t_buf.at[each, part], sem.at[each])
+                relays(each)[part].start()
+
+    def rates(dy):
+        source = (y + 4 - dy) % 4
+        arrived(r_buf.at[rows_of(source, 4)], r_in.at[source])
 
     def updates(dy, other):
         block = ((y + 4 - dy) % 4) * 2 + (z // 2 + other) % 2
@@ -260,41 +260,52 @@
 
     forward(0, 0)
     u_buf[...] = jnp.zeros_like(u_buf)
-    relay(0)
-    relay(1)
+    for source in range(4):
+        arrived(rt_buf.at[source], rt_in.at[source])
+    for dy in TURNS:
+        r_relay(dy).start()
+    pltpu.make_async_copy(rt_buf.at[:, y], r_buf.at[rows_of(y, 4)], r_in.at[y]).start()
+    relay(0, 1)
     forward(1, 0)
     forward(3, 0)
-    relay(2)
-    relay(3)
+    relay(2, 3)
     forward(2, 0)
-    relay(4)
-    relay(5)
+    relay(4, 5)
     forward(1, -1)
     forward(3, -1)
+    forward(1, 1)
+    forward(3, 1)
     forward(0, -1)
     forward(0, 1)
+    for slot in range(6, len(SLOTS)):
+        for copy in slot_sends(slot):
+            copy.start()
+    for copy in kv_sends(straight[5]):
+        copy.start()
+    for dy in range(4):
+        rates(dy)
     updates(0, 0)
-    forward(1, 1)
-    forward(3, 1)
     updates(1, 0)
     relay(6)
     updates(3, 0)
+    forward(2, -1)
+    forward(2, 1)
     relay(7)
-    forward(2, -1)
+    updates(2, 0)
     relay(8)
     pltpu.make_async_copy(columns(q_hbm, me), q_buf.at[mine], q_in.at[me]).start()
-    for peer in peers:
+    for peer in near_peers:
         q_send(peer).start()
-    forward(2, 1)
-    updates(2, 0)
     forward(1, 2)
     updates(1, 1)
     forward(3, 2)
     updates(3, 1)
-    forward(2, 2)
-    updates(2, 1)
     forward(0, 2)
     updates(0, 1)
+    forward(2, 2)
+    for peer in far_peers:
+        q_send(peer).start()
+    updates(2, 1)
 
     def u_send(line):
         return remote(ub_buf.at[line], u_in.at[ctx], u_sent.at[line], u_got.at[ctx], (line, me))
@@ -323,19 +334,53 @@
     def o_local():
         return pltpu.make_async_copy(o_buf.at[mine], columns(out_hbm, me), o_in.at[me])
 
-    def finish(block):
+    def o_slot(dy, dz):
+        return (dz - 1) * 3 + dy - 1
+
+    def o_aside(source, slot):
+        there = o_in_slot.at[slot]
+        here = rows_of(source, ROWS)
+        return remote(o_buf.at[here], there, ot_sent.at[slot], ot_in.at[slot], (ctx, y * 4 + source % 4))
+
+    def o_relay(dy, from_z, slot):
+        there = columns(out_hbm, y * 4 + from_z)
+        peer = ((y + dy) % 4) * 4 + z
+        return remote(o_in_slot.at[slot], there, oa_sent.at[slot], o_in.at[y * 4 + from_z], (ctx, peer))
+
+    def finish(step):
+        back, _ = turn_at(step)
+        dy = (4 - back) % 4
+        block = block_at(step)
         for head in range(2):
             recall(block, head, q_buf, f_buf, a_buf, o_buf)
         for half in range(2):
             source = 2 * block + half
+            dz = (source + 4 - z) % 4
 
             @pl.when(source == me)
             def _():
                 o_local().start()
 
-            @pl.when(source != me)
+            @pl.when(jnp.logical_and(source != me, dy * dz == 0))
             def _():
                 o_send(source).start()
+
+            @pl.when(dy * dz != 0)
+            def _():
+                o_aside(source, o_slot(dy, dz)).start()
+
+    def pass_on(step):
+        back, other = turn_at(step)
+        dy = (4 - back) % 4
+        for half in range(2):
+            from_z = 2 * ((z // 2 + other) % 2) + half
+            dz = (z + 4 - from_z) % 4
+
+            @pl.when(dy * dz != 0)
+            def _():
+                slot = o_slot(dy, dz)
+                arrived(o_in_slot.at[slot], ot_in.at[slot])
+                o_relay(dy, from_z, slot).start()
 
     @pl.loop(0, BLOCKS)
     def _(step):
@@ -367,12 +412,23 @@
 
             @pl.loop(0, FIT_STEP)
             def _(past):
-                finish(block_at(past))
+                finish(past)
 
         @pl.when(step >= FIT_STEP)
         def _():
-            finish(block)
-
+            finish(step)
+
+        @pl.when(step > FIT_STEP)
+        def _():
+            pass_on(step - FIT_STEP - 1)
+
+    @pl.loop(BLOCKS - FIT_STEP - 1, BLOCKS - 2)
+    def _(step):
+        pass_on(step)
+
+    for turn in TURNS:
+        r_aside(turn).wait_send()
+        r_relay(turn).wait_send()
     for peer in straight:
         for copy in kv_sends(peer):
             copy.wait_send()
@@ -380,7 +436,6 @@
         for copy in slot_sends(slot) + relays(slot):
             copy.wait_send()
     for peer in peers:
-        r_send(peer).wait_send()
         q_send(peer).wait_send()
     for line in lines:
         u_send(line).wait_send()
@@ -391,8 +446,14 @@
         for copy in forwards(source):
             copy.wait_send()
 
+    for peer in straight:
+        o_send(peer).wait_send()
+    for dy, dz in OFFSETS:
+        if dy * dz:
+            slot = o_slot(dy, dz)
+            o_aside(device_at(dy, dz), slot).wait_send()
+            o_relay(dy, (z + 4 - dz) % 4, slot).wait_send()
     for peer in peers:
-        o_send(peer).wait_send()
         arrived(columns(out_hbm, peer), o_in.at[peer])
     arrived(columns(out_hbm, me), o_in.at[me])
 
@@ -404,7 +465,7 @@
 
 
 def on_device(queries, keys, values, rates, fast_init, gain):
-    rate_rows = jnp.pad(rates.astype(F32).T.reshape(PEERS, 2, ROWS), ((0, 0), (0, 6), (0, 0)))
+    rate_rows = jnp.pad(rates.astype(F32).T.reshape(4, 4, 2, ROWS), ((0, 0), (0, 0), (0, 6), (0, 0)))
     anywhere = pl.BlockSpec(memory_space=pl.ANY)
     near = pl.BlockSpec(memory_space=pltpu.VMEM)
     dma = pltpu.SemaphoreType.DMA
@@ -418,10 +479,12 @@
             pltpu.VMEM((2 * GROUP, COLS), BF16),
             pltpu.VMEM((2 * GROUP, COLS), BF16),
             pltpu.VMEM((len(SLOTS), 2, ROWS, COLS), BF16),
+            pltpu.VMEM((4, 4, 8, ROWS), F32),
             pltpu.VMEM((PEERS, 8, ROWS), F32),
             pltpu.VMEM((2, BLOCK, GROUP), F32),
             pltpu.VMEM((GROUP, COLS), F32),
             pltpu.VMEM((GROUP, COLS), BF16),
+            pltpu.VMEM((len(SLOTS), ROWS, COLS), BF16),
             pltpu.VMEM((6 * HD, HD), F32),
             pltpu.VMEM((CTX, SLICE, HD), BF16),
             pltpu.VMEM((CTX, SLICE, HD), BF16),
@@ -429,16 +492,17 @@
             pltpu.VMEM((6 * HD, HD), BF16),
             pltpu.VMEM((6, HD, HD), BF16),
         ]
-        + [dma((PEERS,))] * 10
+        + [dma((PEERS,))] * 8
+        + [dma((4,))] * 4
         + [dma((PEERS,))] * 4
-        + [dma((len(SLOTS),))] * 5
+        + [dma((len(SLOTS),))] * 9
         + [dma((CTX,))] * 4,
         compiler_params=pltpu.CompilerParams(
             collective_id=0, has_side_effects=True, vmem_limit_bytes=60 * 2**20
         ),
         name="layer",
     )(queries, keys, values, rate_rows, fast_init)
-    tile = 32
+    tile = 64
     return pl.pallas_call(
         norm_kernel,
         grid=(ROWS // tile,),

time: 131 us -> 127 us (0.969)
  Pallas kernels: 128 us -> 124 us
    pallas_call x1, Pallas kernels: 124 us -> 121 us  [on_device(): pl.pallas_call(main_kernel, out_shape=jax.ShapeDtypeStruct((ROWS, PEERS *...]
where the time goes in v3:
time: 127 us; the launch traced here: 126 us
  Pallas kernels  124 us (98%)
  other arithmetic  1.33 us (1%)
    pallas_call x1, Pallas kernels, on_device(): pl.pallas_call(main_kernel, out_shape=jax.ShapeDtypeStruct((ROWS, PEERS *...  121 us
    pallas_call x1, Pallas kernels, on_device(): pl.pallas_call(norm_kernel, grid=(ROWS // tile,), out_shape=jax.ShapeDtyp...  3.5 us

profile of v3, /device:TPU:4, one launch (start us, length us, event | category | flops | bytes accessed | tf_op | source)
XLA Modules:
  0.0 125.6 jit_solution(11512415855044425789)
XLA Ops:
  0.0 1.3 %pad_convert_fusion.r_hbm = f32[4,4,8,128]{3,2,1,0:T(8,128)} fusion(bf16[4,4,2,128]{3,2,1,0:T(2,128)(2,1)} %bitcast.5), kind=kLoop, calls=%fused_computation | loop fusion | flops 16384 | bytes 73728 | tf_op jit(solution)/shard_map/jit(_pad)/pad | solution.py:468
  1.3 120.7 %layer.1.x_ref = bf16[128,8192]{1,0:T(8,128)(2,1)} custom-call(bf16[128,8192]{1,0:T(8,128)(2,1)} %q_hbm.1, bf16[128,8192]{1,0:T(8,128)(2,1)} %k_hbm.1, bf16[128,8192]{1,0:T(8,128)(2,1)} %v_hbm.1, f32[4,4,8,128]{3,2,1,0:T(8,128)} %pad_convert_fusion.r_hbm, bf16[3,2,256,256]{3,2,1,0:T(8,128)(2,1)} %w_ref.1), custom_call_target="tpu_custom_call" | custom-call | tf_op jit(solution)/shard_map/layer/pallas_call | solution.py:472
  122.1 3.5 %norm.1 = bf16[128,8192]{1,0:T(8,128)(2,1)} custom-call(bf16[128,8192]{1,0:T(8,128)(2,1)} %layer.1.x_ref, f32[1,8192]{1,0:T(1,128)} %bitcast.4), custom_call_target="tpu_custom_call" | custom-call | tf_op jit(solution)/shard_map/norm/pallas_call | solution.py:506

commit v4 on v3

--- a/solution.py
+++ b/solution.py
@@ -26,8 +26,8 @@
 SLICE = 6 * HD // CTX
 SCALE = HD**-0.5 * 1.4426950408889634
 LOW = -1e30
-SUM_STEP = 1
-FIT_STEP = 3
+SUM_STEP = 0
+FIT_STEP = 2
 
 TURNS = (1, 3, 2)
 
@@ -102,7 +102,8 @@
     here = rows_of(block, BLOCK, GROUP)
     key = k_buf[here, cols]
     value = v_buf[here, cols]
-    rate = jnp.concatenate([r_buf[2 * block].T, r_buf[2 * block + 1].T], 0)[:, head : head + 1]
+    lines = [r_buf[2 * block + half].astype(F32)[head : head + 1] for half in range(2)]
+    rate = jnp.concatenate([jnp.broadcast_to(line, (8, ROWS)).T for line in lines], 0)[:, :1]
     target = (rate * value.astype(F32)).astype(BF16)
     gate = dot(key, w_ref[0, head], NT)
     up = dot(key, w_ref[1, head], NT)
@@ -127,7 +128,8 @@
 
 
 def main_kernel(
-    q_hbm, k_hbm, v_hbm, r_hbm, w_ref, out_hbm,
+    q_hbm, k_hbm, v_hbm, r_hbm, w_hbm, out_hbm,
+    w_ref, w_in,
     q_buf, k_buf, v_buf, t_buf, rt_buf, r_buf, s_buf, a_buf, o_buf, o_in_slot, u_buf, ub_buf, u_in, p_out, p_buf, f_buf,
     q_in, k_in, v_in, o_in, q_sent, k_sent, v_sent, o_sent, rt_in, rt_sent, r_in, r_sent,
     fk_in, fv_in, fk_sent, fv_sent, t_in, tv_in, tk_sent, tv_sent, ak_sent, av_sent, ot_in, ot_sent, oa_sent, u_got, u_sent, p_got, p_sent,
@@ -145,6 +147,8 @@
         pl.semaphore_signal(barrier, inc=1, device_id=(ctx, peer), device_id_type=MESH)
     for line in lines:
         pl.semaphore_signal(barrier, inc=1, device_id=(line, me), device_id_type=MESH)
+    weights = pltpu.make_async_copy(w_hbm, w_ref, w_in)
+    weights.start()
     pl.semaphore_wait(barrier, len(peers) + len(lines))
 
     def remote(src, dst, sent, got, where):
@@ -282,6 +286,7 @@
             copy.start()
     for copy in kv_sends(straight[5]):
         copy.start()
+    weights.wait()
     for dy in range(4):
         rates(dy)
     updates(0, 0)
@@ -465,22 +470,23 @@
 
 
 def on_device(queries, keys, values, rates, fast_init, gain):
-    rate_rows = jnp.pad(rates.astype(F32).T.reshape(4, 4, 2, ROWS), ((0, 0), (0, 0), (0, 6), (0, 0)))
+    rate_rows = rates.T.reshape(4, 4, 2, ROWS)
     anywhere = pl.BlockSpec(memory_space=pl.ANY)
-    near = pl.BlockSpec(memory_space=pltpu.VMEM)
     dma = pltpu.SemaphoreType.DMA
     wide = pl.pallas_call(
         main_kernel,
         out_shape=jax.ShapeDtypeStruct((ROWS, PEERS * COLS), BF16),
-        in_specs=[anywhere, anywhere, anywhere, anywhere, near],
+        in_specs=[anywhere] * 5,
         out_specs=anywhere,
         scratch_shapes=[
+            pltpu.VMEM((3, 2, HD, HD), BF16),
+            dma(()),
             pltpu.VMEM((GROUP, COLS), BF16),
             pltpu.VMEM((2 * GROUP, COLS), BF16),
             pltpu.VMEM((2 * GROUP, COLS), BF16),
             pltpu.VMEM((len(SLOTS), 2, ROWS, COLS), BF16),
-            pltpu.VMEM((4, 4, 8, ROWS), F32),
-            pltpu.VMEM((PEERS, 8, ROWS), F32),
+            pltpu.VMEM((4, 4, 2, ROWS), BF16),
+            pltpu.VMEM((PEERS, 2, ROWS), BF16),
             pltpu.VMEM((2, BLOCK, GROUP), F32),
             pltpu.VMEM((GROUP, COLS), F32),
             pltpu.VMEM((GROUP, COLS), BF16),
@@ -498,7 +504,7 @@
         + [dma((len(SLOTS),))] * 9
         + [dma((CTX,))] * 4,
         compiler_params=pltpu.CompilerParams(
-            collective_id=0, has_side_effects=True, vmem_limit_bytes=60 * 2**20
+            collective_id=0, has_side_effects=True, vmem_limit_bytes=67_043_328
         ),
         name="layer",
     )(queries, keys, values, rate_rows, fast_init)

time: 127 us -> 123 us (0.969)
  Pallas kernels: 124 us -> 121 us
  other arithmetic: 1.33 us -> 0 us
    pallas_call x1, Pallas kernels: 121 us -> 118 us  [on_device(): pl.pallas_call(main_kernel, out_shape=jax.ShapeDtypeStruct((ROWS, PEERS *...]
    pad x1 -> x0, other arithmetic: 1.33 us -> none  [on_device(): jnp.pad(rates.astype(F32).T.reshape(4, 4, 2, ROWS), ((0, 0), (0, 0), (0,...]
where the time goes in v4:
time: 123 us; the launch traced here: 121 us
  Pallas kernels  121 us (98%)
    pallas_call x1, Pallas kernels, on_device(): pl.pallas_call(main_kernel, out_shape=jax.ShapeDtypeStruct((ROWS, PEERS *...  118 us
    pallas_call x1, Pallas kernels, on_device(): pl.pallas_call(norm_kernel, grid=(ROWS // tile,), out_shape=jax.ShapeDtyp...  3.5 us

profile of v4, /device:TPU:4, one launch (start us, length us, event | category | flops | bytes accessed | tf_op | source)
XLA Modules:
  0.0 121.5 jit_solution(11577617695541784721)
XLA Ops:
  0.0 118.0 %layer.1.x_ref = bf16[128,8192]{1,0:T(8,128)(2,1)} custom-call(bf16[128,8192]{1,0:T(8,128)(2,1)} %q_hbm.1, bf16[128,8192]{1,0:T(8,128)(2,1)} %k_hbm.1, bf16[128,8192]{1,0:T(8,128)(2,1)} %v_hbm.1, bf16[4,4,2,128]{3,2,1,0:T(2,128)(2,1)} %bitcast.5, bf16[3,2,256,256]{3,2,1,0:T(8,128)(2,1)} %w_hbm.1), custom_call_target="tpu_custom_call" | custom-call | tf_op jit(solution)/shard_map/layer/pallas_call | solution.py:476
  118.0 3.5 %norm.1 = bf16[128,8192]{1,0:T(8,128)(2,1)} custom-call(bf16[128,8192]{1,0:T(8,128)(2,1)} %layer.1.x_ref, f32[1,8192]{1,0:T(1,128)} %bitcast.4), custom_call_target="tpu_custom_call" | custom-call | tf_op jit(solution)/shard_map/norm/pallas_call | solution.py:512

commit v5 on v4

--- a/solution.py
+++ b/solution.py
@@ -464,9 +464,18 @@
 
 
 def norm_kernel(x_ref, gain_ref, out_ref):
-    wide = x_ref[...].astype(F32)
-    factor = lax.rsqrt(jnp.mean(wide * wide, axis=1, keepdims=True) + EPSILON)
-    out_ref[...] = (wide * factor * gain_ref[...]).astype(BF16)
+    strip, lanes = 16, 128
+    for top in range(0, x_ref.shape[0], strip):
+        rows = slice(top, top + strip)
+        squares = jnp.zeros((strip, lanes), F32)
+        for left in range(0, x_ref.shape[1], lanes):
+            part = x_ref[rows, left : left + lanes].astype(F32)
+            squares = squares + part * part
+        mean = jnp.sum(squares, axis=1, keepdims=True) / x_ref.shape[1]
+        factor = lax.rsqrt(mean + EPSILON)
+        for left in range(0, x_ref.shape[1], lanes):
+            cols = slice(left, left + lanes)
+            out_ref[rows, cols] = (x_ref[rows, cols].astype(F32) * factor * gain_ref[:, cols]).astype(BF16)
 
 
 def on_device(queries, keys, values, rates, fast_init, gain):

time: 123 us -> 123 us (level)
  no operation moved by 1% of the time
where the time goes in v5:
time: 123 us; the launch traced here: 121 us
  Pallas kernels  121 us (98%)
    pallas_call x1, Pallas kernels, on_device(): pl.pallas_call(main_kernel, out_shape=jax.ShapeDtypeStruct((ROWS, PEERS *...  118 us
    pallas_call x1, Pallas kernels, on_device(): pl.pallas_call(norm_kernel, grid=(ROWS // tile,), out_shape=jax.ShapeDtyp...  3.24 us

profile of v5, /device:TPU:4, one launch (start us, length us, event | category | flops | bytes accessed | tf_op | source)
XLA Modules:
  0.0 121.2 jit_solution(1086368327607174079)
XLA Ops:
  0.0 118.0 %layer.1.x_ref = bf16[128,8192]{1,0:T(8,128)(2,1)} custom-call(bf16[128,8192]{1,0:T(8,128)(2,1)} %q_hbm.1, bf16[128,8192]{1,0:T(8,128)(2,1)} %k_hbm.1, bf16[128,8192]{1,0:T(8,128)(2,1)} %v_hbm.1, bf16[4,4,2,128]{3,2,1,0:T(2,128)(2,1)} %bitcast.5, bf16[3,2,256,256]{3,2,1,0:T(8,128)(2,1)} %w_hbm.1), custom_call_target="tpu_custom_call" | custom-call | tf_op jit(solution)/shard_map/layer/pallas_call | solution.py:485
  118.0 3.2 %norm.1 = bf16[128,8192]{1,0:T(8,128)(2,1)} custom-call(bf16[128,8192]{1,0:T(8,128)(2,1)} %layer.1.x_ref, f32[1,8192]{1,0:T(1,128)} %bitcast.4), custom_call_target="tpu_custom_call" | custom-call | tf_op jit(solution)/shard_map/norm/pallas_call | solution.py:521
